TPU v7x, 256 devices: a whole 4x4x8 slice. The times are simulated.
256 devices in a mesh: facet: 16 (over x, y), span: 16 (over z, core).
Axes of the slice: x: 4, y: 4, z: 8, core: 2. Of those that a mesh axis runs over, the one named last changes fastest.
Arguments:
- visibilities: bfloat16 [16, 512, 2, 1024], P('span', 'facet'), may hold values from -6 to 6
- coordinates: bfloat16 [16, 512, 2, 1024], P('span', 'facet'), may hold values from 4 to 124
- phases: float32 [16, 512, 1024], P('span', 'facet'), may hold values from -3.140625 to 3.140625
- sub_index: int32 [16, 512], replicated, may hold values from 0 to 4095, as said below
Outputs:
- dirty: float32 [8192, 8192], P(('facet', 'span'))
Inputs may be any that keep to these rules, and one draw needn't show every extreme that they name: `sub_index`: within one span (one row) all 512 subgrid indices differ. A grid block is the set of subgrids with rows f * 4 to (f + 1) * 4 - 1 and columns j * 4 to (j + 1) * 4 - 1 for f < 16, j < 16; at most 4 indices of one row fall in one grid block, and in every row some grid block holds exactly 4 of them.
All inputs are finite; a program needn't handle non-finite values.
Results may differ from a plain program's by a relative error of at most 0.005.
Values may be sent and summed in bfloat16 or wider, within the bound.
No kernel may reach another device: no remote copies, remote signals or barrier semaphores. Data moves between devices by JAX's collectives and lax.ppermute only.
A program may use at most 64 MiB of HBM per device.

v0:
```python
import jax
import jax.numpy as jnp
from jax import lax
from jax.sharding import PartitionSpec as P

N = 8192
P_SIZE = 128
CAP = 4
spread = 0.75


def kernel_rows(positions, cell_index):
    gap_size = cell_index - positions[..., None]
    return jnp.exp(-(gap_size * gap_size) / (2.0 * spread * spread))


def subgrids_of(vis_items, coord_items):
    cell_index = jnp.arange(P_SIZE, dtype=jnp.float32)
    coord_vals = coord_items.astype(jnp.float32)
    row_kernel = kernel_rows(coord_vals[:, 0, :], cell_index)
    col_kernel = kernel_rows(coord_vals[:, 1, :], cell_index).astype(jnp.bfloat16)
    weighted = (vis_items.astype(jnp.float32)[:, :, :, None] * row_kernel[:, None, :, :]).astype(
        jnp.bfloat16
    )
    result = jnp.einsum("ezkp,ekq->ezpq", weighted, col_kernel, preferred_element_type=jnp.float32)
    return result.astype(jnp.bfloat16)


def group_subgrids(group_inputs):
    return subgrids_of(group_inputs[0], group_inputs[1])


def entries(sub_row, target, band_sub, col_sub, span_count):
    side_count = N // P_SIZE
    sub_rows = sub_row // side_count
    sub_cols = sub_row % side_count
    owning_block = sub_rows // band_sub * span_count + sub_cols // col_sub
    local_slot = sub_rows % band_sub * col_sub + sub_cols % col_sub
    inside = (owning_block == target).astype(jnp.int32)
    rank_of = jnp.cumsum(inside) - 1
    picked = (
        (inside[None, :] == 1) & (rank_of[None, :] == jnp.arange(CAP, dtype=jnp.int32)[:, None])
    ).astype(jnp.int32)
    block_num = jnp.arange(sub_row.shape[0], dtype=jnp.int32)
    block_ids = jnp.sum(picked * block_num[None, :], axis=1)
    slot_ids = jnp.sum(picked * local_slot[None, :], axis=1)
    filled = jnp.sum(picked, axis=1) > 0
    return (block_ids, slot_ids, filled)


def phase_table(row_count, col_count, length):
    row_ids = jnp.arange(row_count, dtype=jnp.int32)[:, None]
    col_ids = jnp.arange(col_count, dtype=jnp.int32)[None, :]
    angles = 2.0 * jnp.pi / length * (row_ids * col_ids % length).astype(jnp.float32)
    return (jnp.cos(angles), jnp.sin(angles))


def inverse_dft(real_part, imag_part):
    length = real_part.shape[-1]
    first_len = 64
    second_len = length // first_len
    leading = real_part.shape[:-1]
    split_real = real_part.reshape(leading + (first_len, second_len))
    split_imag = imag_part.reshape(leading + (first_len, second_len))
    highest = lax.Precision.HIGHEST
    cos_first, sin_first = phase_table(first_len, first_len, first_len)
    step_real = jnp.einsum(
        "av,...vb->...ab", cos_first, split_real, precision=highest
    ) - jnp.einsum("av,...vb->...ab", sin_first, split_imag, precision=highest)
    step_imag = jnp.einsum(
        "av,...vb->...ab", cos_first, split_imag, precision=highest
    ) + jnp.einsum("av,...vb->...ab", sin_first, split_real, precision=highest)
    cos_twist, sin_twist = phase_table(first_len, second_len, length)
    twist_real = step_real * cos_twist - step_imag * sin_twist
    twist_imag = step_real * sin_twist + step_imag * cos_twist
    cos_second, sin_second = phase_table(second_len, second_len, second_len)
    out_real = jnp.einsum(
        "...ab,bc->...ac", twist_real, cos_second, precision=highest
    ) - jnp.einsum("...ab,bc->...ac", twist_imag, sin_second, precision=highest)
    out_imag = jnp.einsum(
        "...ab,bc->...ac", twist_real, sin_second, precision=highest
    ) + jnp.einsum("...ab,bc->...ac", twist_imag, cos_second, precision=highest)
    out_real = jnp.swapaxes(out_real, -1, -2).reshape(leading + (length,))
    out_imag = jnp.swapaxes(out_imag, -1, -2).reshape(leading + (length,))
    return (out_real, out_imag)


def shards(visibilities, coordinates, phases, sub_index):
    facet_count = lax.axis_size("facet")
    span_count = lax.axis_size("span")
    side_count = N // P_SIZE
    band_sub = side_count // facet_count
    col_sub = side_count // span_count
    facet_id = lax.axis_index("facet")
    span_id = lax.axis_index("span")
    vis_count = visibilities.shape[3]
    vis_float = visibilities.astype(jnp.float32)
    cosine = jnp.cos(phases)
    sine = jnp.sin(phases)
    real_part = vis_float[:, :, 0, :]
    imag_part = vis_float[:, :, 1, :]
    rotated = jnp.stack(
        [real_part * cosine - imag_part * sine, real_part * sine + imag_part * cosine], axis=2
    ).astype(jnp.bfloat16)
    own_row = lax.dynamic_index_in_dim(sub_index, span_id, 0, keepdims=False)
    targets = facet_id * span_count + jnp.arange(span_count, dtype=jnp.int32)

    def send_table(target):
        return entries(own_row, target, band_sub, col_sub, span_count)

    send_ids, send_slots, send_filled = jax.vmap(send_table)(targets)
    flat_ids = send_ids.reshape(-1)
    flat_filled = send_filled.reshape(-1)
    entry_count = flat_ids.shape[0]
    blank = jnp.zeros((entry_count, 2, vis_count), jnp.bfloat16)
    pieces = (
        lax.all_gather(rotated, "facet", axis=1, tiled=True),
        lax.all_gather(coordinates, "facet", axis=1, tiled=True),
    )
    rows_here = pieces[0].shape[1]
    inside = flat_filled & (flat_ids >= 0) & (flat_ids < rows_here)
    where_row = jnp.clip(flat_ids, 0, rows_here - 1)
    vis_rows = jnp.take(pieces[0][0], where_row, axis=0)
    coord_rows = jnp.take(pieces[1][0], where_row, axis=0)
    keep_mask = inside[:, None, None]
    chosen_vis = jnp.where(keep_mask, vis_rows, blank)
    chosen_coords = jnp.where(keep_mask, coord_rows, blank)
    grouped_vis = chosen_vis.reshape(span_count, CAP, 2, vis_count)
    grouped_coords = chosen_coords.reshape(span_count, CAP, 2, vis_count)
    made_subs = lax.map(group_subgrids, (grouped_vis, grouped_coords))
    arrived = lax.all_to_all(made_subs, "span", split_axis=0, concat_axis=0, tiled=True)
    my_block = facet_id * span_count + span_id

    def recv_table(source_row):
        return entries(source_row, my_block, band_sub, col_sub, span_count)

    recv_ids, recv_slots, recv_filled = jax.vmap(recv_table)(sub_index)
    slots_here = band_sub * col_sub
    slot_range = jnp.arange(slots_here, dtype=jnp.int32)[:, None]
    onehot = (
        (recv_slots.reshape(-1)[None, :] == slot_range) & recv_filled.reshape(-1)[None, :]
    ).astype(jnp.bfloat16)
    items = arrived.reshape(span_count * CAP, 2 * P_SIZE * P_SIZE)
    summed = jnp.dot(onehot, items, preferred_element_type=jnp.float32)
    block = (
        summed.reshape(band_sub, col_sub, 2, P_SIZE, P_SIZE)
        .transpose(2, 0, 3, 1, 4)
        .reshape(2, band_sub * P_SIZE, col_sub * P_SIZE)
    )
    row_block = lax.all_to_all(block, "span", split_axis=1, concat_axis=2, tiled=True)
    half_real, half_imag = inverse_dft(row_block[0], row_block[1])
    half_done = jnp.stack([half_real, half_imag])
    columns = lax.all_to_all(
        lax.all_to_all(half_done, "facet", split_axis=2, concat_axis=1, tiled=True),
        "span",
        split_axis=2,
        concat_axis=1,
        tiled=True,
    )
    row_count = half_done.shape[1]
    col_count = columns.shape[2]
    ordered = (
        columns.reshape(2, span_count, facet_count, row_count, col_count)
        .transpose(0, 4, 2, 1, 3)
        .reshape(2, col_count, N)
    )
    image_real, image_imag = inverse_dft(ordered[0], ordered[1])
    return image_real * (1.0 / N)


def solution(mesh):
    return jax.shard_map(
        shards,
        mesh=mesh,
        in_specs=(
            P("span", "facet", None, None),
            P("span", "facet", None, None),
            P("span", "facet", None),
            P(),
        ),
        out_specs=P(("facet", "span"), None),
        check_vma=False,
    )
```

profile of v0, /device:TPU:1, one launch (start us, length us, event | category | flops | bytes accessed | tf_op | source)
XLA Modules:
  0.0 588.6 jit_solution(86421095488678001)
XLA Ops:
  12.9 49.8 %all-gather.5.cloned.1.call-done = bf16[1,512,2,1024]{3,2,0,1:T(2,128)(2,1)} async-done(((bf16[1,32,2,1024]{3,2,0,1:T(2,128)(2,1)}), bf16[1,512,2,1024]{3,2,0,1:T(2,128)(2,1)}) %all-gather.5.cloned.1.call-update) | async-done | bytes 2097168 | tf_op jit(solution)/shard_map/all_gather | solution.py:118
  65.4 49.1 %all-gather.3.cloned.1.call-done = bf16[1,512,2,1024]{3,2,0,1:T(2,128)(2,1)} async-done(((bf16[1,32,2,1024]{3,2,0,1:T(2,128)(2,1)}), bf16[1,512,2,1024]{3,2,0,1:T(2,128)(2,1)}) %all-gather.3.cloned.1.call-update) | async-done | bytes 2097168 | tf_op jit(solution)/shard_map/all_gather | solution.py:117
  117.9 90.2 %while.10 = (s32[]{:T(128)}, bf16[16,4,2,128,128]{4,3,2,1,0:T(8,128)(2,1)}, bf16[16,4,2,1024]{3,2,1,0:T(2,128)(2,1)S(1)}, bf16[16,4,2,1024]{3,2,1,0:T(2,128)(2,1)S(1)}, s32[]{:T(128)}) while((s32[]{:T(128)}, bf16[16,4,2,128,128]{4,3,2,1,0:T(8,128)(2,1)}, bf16[16,4,2,1024]{3,2,1,0:T(2,128)(2,1)S(1)}, bf16[16,4,2,1024]{3,2,1,0:T(2,128)(2,1)S(1)}, ...), condition=%wide.region_9.11_spmd, body=%wide.region_8.10_spmd.sunk | while | flops 275398656 | bytes 8912977 | solution.py:130
  137.4 3.1 fusion.190
  208.1 8.5 %all-to-all-start = ((bf16[16,4,2,128,128]{4,3,2,1,0:T(8,128)(2,1)}), bf16[16,4,2,128,128]{4,3,2,1,0:T(8,128)(2,1)}, u32[]{:S(2)}, u32[]{:S(2)}) async-start(bf16[16,4,2,128,128]{4,3,2,1,0:T(8,128)(2,1)} %get-tuple-element.28), calls=%async_computation | async-start | bytes 8388608 | tf_op jit(solution)/shard_map/all_to_all | solution.py:131
  218.9 91.3 %all-to-all-done = bf16[16,4,2,128,128]{4,3,2,1,0:T(8,128)(2,1)} async-done(((bf16[16,4,2,128,128]{4,3,2,1,0:T(8,128)(2,1)}), bf16[16,4,2,128,128]{4,3,2,1,0:T(8,128)(2,1)}, u32[]{:S(2)}, u32[]{:S(2)}) %all-to-all-start) | async-done | bytes 4194336 | tf_op jit(solution)/shard_map/all_to_all | solution.py:131
  310.2 7.3 %reshape.280 = bf16[64,32768]{1,0:T(8,128)(2,1)} reshape(bf16[16,4,2,128,128]{4,3,2,1,0:T(8,128)(2,1)} %all-to-all-done) | data formatting | bytes 8388608 | tf_op jit(solution)/shard_map/reshape | solution.py:143
  317.5 3.3 copy.148
  326.5 5.8 all-to-all-start.1
  332.4 48.7 %all-to-all-done.1 = f32[2,512,512]{2,0,1:T(2,128)S(1)} async-done(((f32[2,512,512]{2,0,1:T(2,128)}), f32[2,512,512]{2,0,1:T(2,128)S(1)}, u32[]{:S(2)}, u32[]{:S(2)}) %all-to-all-start.1) | async-done | bytes 2097184 | tf_op jit(solution)/shard_map/all_to_all | solution.py:150
  397.9 3.4 fusion.23
  406.1 7.9 %copy.130 = f32[2,32,8192]{1,0,2:T(2,128)} copy(f32[2,32,8192]{2,1,0:T(8,128)S(1)} %pad_maximum_fusion) | data formatting | bytes 4194304 | tf_op jit(solution)/shard_map/stack | solution.py:152
  414.0 10.3 %reshape.317 = f32[16,1,32768]{2,1,0:T(1,128)S(1)} reshape(f32[8192,2,32]{2,1,0:T(2,128)} %bitcast.179) | data formatting | bytes 4194304
  424.3 31.8 %all_to_all.53 = f32[16,1,32768]{2,1,0:T(1,128)} all-to-all(f32[16,1,32768]{2,1,0:T(1,128)S(1)} %reshape.317), channel_id=1, replica_groups=mesh['facet'=16,'span'=16] {'facet'}, dimensions={0} | all-to-all | bytes 4194304 | tf_op jit(solution)/shard_map/all_to_all | solution.py:154
  456.6 7.3 %reduce.4 = f32[16,32768]{1,0:T(8,128)S(1)} reduce(f32[16,1,32768]{2,1,0:T(1,128)} %all_to_all.53, f32[]{:T(128)} %broadcast.473), dimensions={1}, to_apply=%all_to_all.42.reduce_sub_computation | reduce | bytes 4194308 | tf_op jit(solution)/shard_map/all_to_all | solution.py:154
  463.9 9.0 %reshape.318 = f32[8192,2,32]{2,1,0:T(2,128)} reshape(f32[16,32768]{1,0:T(8,128)S(1)} %reduce.4) | data formatting | bytes 4194304
  472.9 10.2 %copy.142 = f32[2,32,16,512]{3,1,2,0:T(8,128)S(1)} copy(f32[2,32,16,512]{1,0,3,2:T(2,128)} %bitcast.180) | data formatting | bytes 4194304 | tf_op jit(solution)/shard_map/all_to_all | solution.py:154
  485.6 58.1 %all_to_all.54 = f32[2,512,512]{1,0,2:T(2,128)S(1)} all-to-all(f32[2,512,512]{1,0,2:T(2,128)} %copy.133), channel_id=1, replica_groups=mesh['facet'=16,'span'=16] {'span'}, dimensions={2} | all-to-all | bytes 4194304 | tf_op jit(solution)/shard_map/all_to_all | solution.py:153
  544.0 4.4 reshape.282
  548.5 6.1 %fusion.174 = (f32[1,32,16,16,32]{4,2,1,3,0:T(8,128)S(1)}, f32[1,32,16,16,32]{4,2,1,3,0:T(8,128)}) fusion(f32[2,32,16,16,32]{4,2,1,3,0:T(8,128)} %bitcast.181), kind=kLoop, calls=%fused_computation.251 | loop fusion | bytes 4194304 | tf_op jit(solution)/shard_map/slice | solution.py:167
  554.6 4.4 copy.135
  558.9 3.3 reshape_squeeze.14
  563.4 6.5 %copy.136 = f32[1,32,16,16,32]{4,3,2,1,0:T(8,128)} copy(f32[1,32,16,16,32]{4,2,1,3,0:T(8,128)} %get-tuple-element.70) | data formatting | bytes 2097152 | tf_op jit(solution)/shard_map/slice | solution.py:167
  569.9 3.4 reshape_squeeze.15
  (195 shorter events, 140.9 us)
Async XLA Ops:
  6.5 4.0 copy-start.1
  6.5 56.2 %all-gather.5.cloned.1.call-start = ((), (), s32[]{:S(2)}) async-start(), calls=%async_computation.5 | async-start | bytes 2228224 | tf_op jit(solution)/shard_map/all_gather | solution.py:118
  7.3 107.3 %all-gather.3.cloned.1.call-start = ((), (), s32[]{:S(2)}) async-start(), calls=%async_computation.4 | async-start | bytes 2228224 | tf_op jit(solution)/shard_map/all_gather | solution.py:117
  208.1 102.1 %all-to-all-start = ((bf16[16,4,2,128,128]{4,3,2,1,0:T(8,128)(2,1)}), bf16[16,4,2,128,128]{4,3,2,1,0:T(8,128)(2,1)}, u32[]{:S(2)}, u32[]{:S(2)}) async-start(bf16[16,4,2,128,128]{4,3,2,1,0:T(8,128)(2,1)} %get-tuple-element.28), calls=%async_computation | async-start | bytes 8388608 | tf_op jit(solution)/shard_map/all_to_all | solution.py:131
  326.5 54.6 %all-to-all-start.1 = ((f32[2,512,512]{2,0,1:T(2,128)}), f32[2,512,512]{2,0,1:T(2,128)S(1)}, u32[]{:S(2)}, u32[]{:S(2)}) async-start(f32[2,512,512]{2,0,1:T(2,128)} %reshape.314), calls=%async_computation.1 | async-start | bytes 4194304 | tf_op jit(solution)/shard_map/all_to_all | solution.py:150
  385.3 1.2 copy-start
Sparse Core Ops, SparseCore 0:
  9.8 52.8 all-gather.4
  65.2 49.3 all-gather.2
where the time goes:
time: 598 us; the launch traced here: 589 us
  waiting for transfers between devices  240 us (40%)
  local copies, waits for them, and re-layouts  133 us (22%)
  blocking collectives  89.9 us (15%)
  matrix products  72.7 us (12%)
  other arithmetic  24.1 us (4%)
  starting transfers between devices  14.4 us (2%)
  between operations  14 us (2%)
    all_to_all x1, waiting for transfers between devices, shards(): lax.all_to_all(made_subs, 'span', split_axis=0, concat_axis=0, tiled=True)  91.3 us
    all_to_all x1, blocking collectives, shards(): lax.all_to_all(lax.all_to_all(half_done, 'facet', split_axis=2, concat_ax...  58.1 us
    all_gather x1, waiting for transfers between devices, shards(): lax.all_gather(coordinates, 'facet', axis=1, tiled=True)  49.8 us
    dot_general x16, matrix products, subgrids_of(): jnp.einsum('ezkp,ekq->ezpq', weighted, col_kernel, preferred_element_type...  49.2 us
    all_gather x1, waiting for transfers between devices, shards(): lax.all_gather(rotated, 'facet', axis=1, tiled=True)  49.1 us
    all_to_all x1, waiting for transfers between devices, shards(): lax.all_to_all(block, 'span', split_axis=1, concat_axis=2, tiled=True)  48.7 us
    all_to_all x1, blocking collectives, shards(): lax.all_to_all(half_done, 'facet', split_axis=2, concat_axis=1, tiled=True)  31.8 us
    exp x16, local copies, waits for them, and re-layouts, kernel_rows(): return jnp.exp(-(gap_size * gap_size) / (2.0 * spread * spread))  29.8 us
  transfers between devices with their start and end apart: 4, of which 4 were waited for; matrix products, arithmetic and copies ran while one was open for 2% of the time, Pallas kernels for 0%

commit v1 on v0

--- a/solution.py
+++ b/solution.py
@@ -7,6 +7,22 @@
 P_SIZE = 128
 CAP = 4
 spread = 0.75
+
+
+def gather_around(x, axis, dim):
+    ways, here, hop = (lax.axis_size(axis), lax.axis_index(axis), x.shape[dim])
+    dims = [n * ways if d == dim else n for d, n in enumerate(x.shape)]
+    full = lax.dynamic_update_slice_in_dim(jnp.zeros(dims, x.dtype), x, here * hop, axis=dim)
+    going_up = going_down = x
+    for far in range(1, ways // 2 + 1):
+        going_up = lax.ppermute(going_up, axis, [(d, (d + 1) % ways) for d in range(ways)])
+        full = lax.dynamic_update_slice_in_dim(full, going_up, (here - far) % ways * hop, axis=dim)
+        if 2 * far < ways:
+            going_down = lax.ppermute(going_down, axis, [(d, (d - 1) % ways) for d in range(ways)])
+            full = lax.dynamic_update_slice_in_dim(
+                full, going_down, (here + far) % ways * hop, axis=dim
+            )
+    return full
 
 
 def kernel_rows(positions, cell_index):
@@ -114,7 +130,7 @@
     entry_count = flat_ids.shape[0]
     blank = jnp.zeros((entry_count, 2, vis_count), jnp.bfloat16)
     pieces = (
-        lax.all_gather(rotated, "facet", axis=1, tiled=True),
+        gather_around(rotated, "facet", 1),
         lax.all_gather(coordinates, "facet", axis=1, tiled=True),
     )
     rows_here = pieces[0].shape[1]

time: 598 us -> 576 us (0.963)
  waiting for transfers between devices: 240 us -> 169 us
  starting transfers between devices: 14.4 us -> 62 us
    all_gather x1, waiting for transfers between devices: 49.8 us -> 0.02 us  [shards(): lax.all_gather(coordinates, 'facet', axis=1, tiled=True)]
    all_gather x1 -> x0, waiting for transfers between devices: 49.1 us -> none  [shards(): lax.all_gather(rotated, 'facet', axis=1, tiled=True)]
    ppermute x0 -> x15, starting transfers between devices: none -> 36.9 us  [the longest x7 36.7 us: gather_around(): lax.ppermute(going_down, axis, [(d, (d - 1) % ways) for d in range(ways)])]
    ppermute x0 -> x15, waiting for transfers between devices: none -> 27.3 us  [the longest x8 17.1 us: gather_around(): lax.ppermute(going_up, axis, [(d, (d + 1) % ways) for d in range(ways)])]
    all_to_all x1, starting transfers between devices: 8.52 us -> 19.6 us  [shards(): lax.all_to_all(made_subs, 'span', split_axis=0, concat_axis=0, tiled=True)]
  transfers between devices with their start and end apart: 4 -> 18, of which waited for: 4 -> 13; matrix products, arithmetic and copies ran while one was open for 2% -> 2% of each run, Pallas kernels for 0% -> 0%
where the time goes in v1:
time: 576 us; the launch traced here: 566 us
  waiting for transfers between devices  169 us (29%)
  local copies, waits for them, and re-layouts  134 us (23%)
  blocking collectives  88.4 us (15%)
  matrix products  72.6 us (13%)
  starting transfers between devices  62 us (11%)
  other arithmetic  24.7 us (4%)
  between operations  14.7 us (3%)
    all_to_all x1, waiting for transfers between devices, shards(): lax.all_to_all(made_subs, 'span', split_axis=0, concat_axis=0, tiled=True)  93 us
    all_to_all x1, blocking collectives, shards(): lax.all_to_all(lax.all_to_all(half_done, 'facet', split_axis=2, concat_ax...  58 us
    dot_general x16, matrix products, subgrids_of(): jnp.einsum('ezkp,ekq->ezpq', weighted, col_kernel, preferred_element_type...  49.2 us
    all_to_all x1, waiting for transfers between devices, shards(): lax.all_to_all(block, 'span', split_axis=1, concat_axis=2, tiled=True)  48.8 us
    ppermute x7, starting transfers between devices, gather_around(): lax.ppermute(going_down, axis, [(d, (d - 1) % ways) for d in range(ways)])  36.7 us
    all_to_all x1, blocking collectives, shards(): lax.all_to_all(half_done, 'facet', split_axis=2, concat_axis=1, tiled=True)  30.4 us
    exp x16, local copies, waits for them, and re-layouts, kernel_rows(): return jnp.exp(-(gap_size * gap_size) / (2.0 * spread * spread))  29.7 us
    unnamed x7, local copies, waits for them, and re-layouts  22.7 us
  transfers between devices with their start and end apart: 18, of which 13 were waited for; matrix products, arithmetic and copies ran while one was open for 2% of the time, Pallas kernels for 0%

profile of v1, /device:TPU:1, one launch (start us, length us, event | category | flops | bytes accessed | tf_op | source)
XLA Modules:
  0.0 566.3 jit_solution(11151851214256946612)
XLA Ops:
  9.4 5.8 %collective-permute-start.1 = (bf16[1,32,2,1024]{3,2,1,0:T(2,128)(2,1)S(1)}, bf16[1,32,2,1024]{3,2,1,0:T(2,128)(2,1)S(1)}, u32[]{:S(2)}, u32[]{:S(2)}) collective-permute-start(bf16[1,32,2,1024]{3,2,1,0:T(2,128)(2,1)S(1)} %pad_maximum_fusion.1), channel_id=1, source_target_pairs={{0,240},{16,0},{32,16},{48,32},{64,48},{80,64},{96,80},{112,96},{1... | collective-permute-start | bytes 393224 | tf_op jit(solution)/shard_map/ppermute | solution.py:21
  21.6 4.9 collective-permute-start.3
  28.4 5.2 collective-permute-start.5
  35.5 5.2 collective-permute-start.7
  42.9 5.2 collective-permute-start.9
  50.1 5.2 collective-permute-start.11
  60.5 5.2 collective-permute-start.13
  66.8 7.6 %collective-permute-done.12 = bf16[1,32,2,1024]{3,2,1,0:T(2,128)(2,1)S(1)} collective-permute-done((bf16[1,32,2,1024]{3,2,1,0:T(2,128)(2,1)S(1)}, bf16[1,32,2,1024]{3,2,1,0:T(2,128)(2,1)S(1)}, u32[]{:S(2)}, u32[]{:S(2)}) %collective-permute-start.12) | collective-permute-done | bytes 131104 | tf_op jit(solution)/shard_map/ppermute | solution.py:18
  74.6 6.9 %collective-permute-done.14 = bf16[1,32,2,1024]{3,2,1,0:T(2,128)(2,1)S(1)} collective-permute-done((bf16[1,32,2,1024]{3,2,1,0:T(2,128)(2,1)S(1)}, bf16[1,32,2,1024]{3,2,1,0:T(2,128)(2,1)S(1)}, u32[]{:S(2)}, u32[]{:S(2)}) %collective-permute-start.14) | collective-permute-done | bytes 131104 | tf_op jit(solution)/shard_map/ppermute | solution.py:18
  86.1 90.1 %while.10 = (s32[]{:T(128)}, bf16[16,4,2,128,128]{4,3,2,1,0:T(8,128)(2,1)}, bf16[16,4,2,1024]{3,2,1,0:T(2,128)(2,1)S(1)}, bf16[16,4,2,1024]{3,2,1,0:T(2,128)(2,1)S(1)}, s32[]{:T(128)}) while((s32[]{:T(128)}, bf16[16,4,2,128,128]{4,3,2,1,0:T(8,128)(2,1)}, bf16[16,4,2,1024]{3,2,1,0:T(2,128)(2,1)S(1)}, bf16[16,4,2,1024]{3,2,1,0:T(2,128)(2,1)S(1)}, ...), condition=%wide.region_9.11_spmd, body=%wide.region_8.10_spmd.sunk | while | flops 275398656 | bytes 8912977 | solution.py:146
  176.2 19.6 %all-to-all-start = ((bf16[16,4,2,128,128]{4,3,2,1,0:T(8,128)(2,1)}), bf16[16,4,2,128,128]{4,3,2,1,0:T(8,128)(2,1)}, u32[]{:S(2)}, u32[]{:S(2)}) async-start(bf16[16,4,2,128,128]{4,3,2,1,0:T(8,128)(2,1)} %get-tuple-element.28), calls=%async_computation | async-start | bytes 8388608 | tf_op jit(solution)/shard_map/all_to_all | solution.py:147
  196.2 93.0 %all-to-all-done = bf16[16,4,2,128,128]{4,3,2,1,0:T(8,128)(2,1)} async-done(((bf16[16,4,2,128,128]{4,3,2,1,0:T(8,128)(2,1)}), bf16[16,4,2,128,128]{4,3,2,1,0:T(8,128)(2,1)}, u32[]{:S(2)}, u32[]{:S(2)}) %all-to-all-start) | async-done | bytes 4194336 | tf_op jit(solution)/shard_map/all_to_all | solution.py:147
  289.2 7.3 %reshape.318 = bf16[64,32768]{1,0:T(8,128)(2,1)} reshape(bf16[16,4,2,128,128]{4,3,2,1,0:T(8,128)(2,1)} %all-to-all-done) | data formatting | bytes 8388608 | tf_op jit(solution)/shard_map/reshape | solution.py:159
  305.5 5.5 all-to-all-start.1
  311.1 48.8 %all-to-all-done.1 = f32[2,512,512]{2,0,1:T(2,128)S(1)} async-done(((f32[2,512,512]{2,0,1:T(2,128)}), f32[2,512,512]{2,0,1:T(2,128)S(1)}, u32[]{:S(2)}, u32[]{:S(2)}) %all-to-all-start.1) | async-done | bytes 2097184 | tf_op jit(solution)/shard_map/all_to_all | solution.py:166
  384.9 7.9 %copy.182 = f32[2,32,8192]{1,0,2:T(2,128)} copy(f32[2,32,8192]{2,1,0:T(8,128)S(1)} %pad_maximum_fusion) | data formatting | bytes 4194304 | tf_op jit(solution)/shard_map/stack | solution.py:168
  392.9 10.3 %reshape.355 = f32[16,1,32768]{2,1,0:T(1,128)S(1)} reshape(f32[8192,2,32]{2,1,0:T(2,128)} %bitcast.200) | data formatting | bytes 4194304
  403.2 30.4 %all_to_all.53 = f32[16,1,32768]{2,1,0:T(1,128)} all-to-all(f32[16,1,32768]{2,1,0:T(1,128)S(1)} %reshape.355), channel_id=1, replica_groups=mesh['facet'=16,'span'=16] {'facet'}, dimensions={0} | all-to-all | bytes 4194304 | tf_op jit(solution)/shard_map/all_to_all | solution.py:170
  434.1 7.3 %reduce.4 = f32[16,32768]{1,0:T(8,128)S(1)} reduce(f32[16,1,32768]{2,1,0:T(1,128)} %all_to_all.53, f32[]{:T(128)} %broadcast.490), dimensions={1}, to_apply=%all_to_all.42.reduce_sub_computation | reduce | bytes 4194308 | tf_op jit(solution)/shard_map/all_to_all | solution.py:170
  441.4 9.0 %reshape.356 = f32[8192,2,32]{2,1,0:T(2,128)} reshape(f32[16,32768]{1,0:T(8,128)S(1)} %reduce.4) | data formatting | bytes 4194304
  450.4 10.2 %copy.194 = f32[2,32,16,512]{3,1,2,0:T(8,128)S(1)} copy(f32[2,32,16,512]{1,0,3,2:T(2,128)} %bitcast.201) | data formatting | bytes 4194304 | tf_op jit(solution)/shard_map/all_to_all | solution.py:170
  463.0 58.0 %all_to_all.54 = f32[2,512,512]{1,0,2:T(2,128)S(1)} all-to-all(f32[2,512,512]{1,0,2:T(2,128)} %copy.185), channel_id=1, replica_groups=mesh['facet'=16,'span'=16] {'span'}, dimensions={2} | all-to-all | bytes 4194304 | tf_op jit(solution)/shard_map/all_to_all | solution.py:169
  525.8 6.1 %fusion.172 = (f32[1,32,16,16,32]{4,2,1,3,0:T(8,128)S(1)}, f32[1,32,16,16,32]{4,2,1,3,0:T(8,128)}) fusion(f32[2,32,16,16,32]{4,2,1,3,0:T(8,128)} %bitcast.202), kind=kLoop, calls=%fused_computation.266 | loop fusion | bytes 4194304 | tf_op jit(solution)/shard_map/slice | solution.py:183
  540.7 6.6 %copy.188 = f32[1,32,16,16,32]{4,3,2,1,0:T(8,128)} copy(f32[1,32,16,16,32]{4,2,1,3,0:T(8,128)} %get-tuple-element.78) | data formatting | bytes 2097152 | tf_op jit(solution)/shard_map/slice | solution.py:183
  (241 shorter events, 179.8 us)
Async XLA Ops:
  6.5 8.8 %copy-start.1 = (s32[16,512]{1,0:T(8,128)S(1)}, s32[16,512]{1,0:T(8,128)}, u32[]{:S(2)}) copy-start(s32[16,512]{1,0:T(8,128)} %param.11) | copy-start | bytes 98308
  6.5 76.2 %all-gather.2.cloned.1.call-start = ((), (), s32[]{:S(2)}) async-start(), calls=%async_computation.4 | async-start | bytes 2228224 | tf_op jit(solution)/shard_map/all_gather | solution.py:134
  9.4 12.2 %collective-permute-start.1 = (bf16[1,32,2,1024]{3,2,1,0:T(2,128)(2,1)S(1)}, bf16[1,32,2,1024]{3,2,1,0:T(2,128)(2,1)S(1)}, u32[]{:S(2)}, u32[]{:S(2)}) collective-permute-start(bf16[1,32,2,1024]{3,2,1,0:T(2,128)(2,1)S(1)} %pad_maximum_fusion.1), channel_id=1, source_target_pairs={{0,240},{16,0},{32,16},{48,32},{64,48},{80,64},{96,80},{112,96},{1... | collective-permute-start | bytes 393224 | tf_op jit(solution)/shard_map/ppermute | solution.py:21
  15.3 11.2 %collective-permute-start = (bf16[1,32,2,1024]{3,2,1,0:T(2,128)(2,1)S(1)}, bf16[1,32,2,1024]{3,2,1,0:T(2,128)(2,1)S(1)}, u32[]{:S(2)}, u32[]{:S(2)}) collective-permute-start(bf16[1,32,2,1024]{3,2,1,0:T(2,128)(2,1)S(1)} %pad_maximum_fusion.1), channel_id=1, source_target_pairs={{0,16},{16,32},{32,48},{48,64},{64,80},{80,96},{96,112},{112,128},... | collective-permute-start | bytes 393224 | tf_op jit(solution)/shard_map/ppermute | solution.py:18
  21.6 6.8 %collective-permute-start.3 = (bf16[1,32,2,1024]{3,2,1,0:T(2,128)(2,1)S(1)}, bf16[1,32,2,1024]{3,2,1,0:T(2,128)(2,1)S(1)}, u32[]{:S(2)}, u32[]{:S(2)}) collective-permute-start(bf16[1,32,2,1024]{3,2,1,0:T(2,128)(2,1)S(1)} %collective-permute-done.1), channel_id=1, source_target_pairs={{0,240},{16,0},{32,16},{48,32},{64,48},{80,64},{96,80},{112,96},{1... | collective-permute-start | bytes 393224 | tf_op jit(solution)/shard_map/ppermute | solution.py:21
  26.5 7.1 %collective-permute-start.2 = (bf16[1,32,2,1024]{3,2,1,0:T(2,128)(2,1)S(1)}, bf16[1,32,2,1024]{3,2,1,0:T(2,128)(2,1)S(1)}, u32[]{:S(2)}, u32[]{:S(2)}) collective-permute-start(bf16[1,32,2,1024]{3,2,1,0:T(2,128)(2,1)S(1)} %collective-permute-done), channel_id=1, source_target_pairs={{0,16},{16,32},{32,48},{48,64},{64,80},{80,96},{96,112},{112,128},... | collective-permute-start | bytes 393224 | tf_op jit(solution)/shard_map/ppermute | solution.py:18
  28.4 7.1 %collective-permute-start.5 = (bf16[1,32,2,1024]{3,2,1,0:T(2,128)(2,1)S(1)}, bf16[1,32,2,1024]{3,2,1,0:T(2,128)(2,1)S(1)}, u32[]{:S(2)}, u32[]{:S(2)}) collective-permute-start(bf16[1,32,2,1024]{3,2,1,0:T(2,128)(2,1)S(1)} %collective-permute-done.3), channel_id=1, source_target_pairs={{0,240},{16,0},{32,16},{48,32},{64,48},{80,64},{96,80},{112,96},{1... | collective-permute-start | bytes 393224 | tf_op jit(solution)/shard_map/ppermute | solution.py:21
  33.6 7.8 %collective-permute-start.4 = (bf16[1,32,2,1024]{3,2,1,0:T(2,128)(2,1)S(1)}, bf16[1,32,2,1024]{3,2,1,0:T(2,128)(2,1)S(1)}, u32[]{:S(2)}, u32[]{:S(2)}) collective-permute-start(bf16[1,32,2,1024]{3,2,1,0:T(2,128)(2,1)S(1)} %collective-permute-done.2), channel_id=1, source_target_pairs={{0,16},{16,32},{32,48},{48,64},{64,80},{80,96},{96,112},{112,128},... | collective-permute-start | bytes 393224 | tf_op jit(solution)/shard_map/ppermute | solution.py:18
  35.5 7.4 %collective-permute-start.7 = (bf16[1,32,2,1024]{3,2,1,0:T(2,128)(2,1)S(1)}, bf16[1,32,2,1024]{3,2,1,0:T(2,128)(2,1)S(1)}, u32[]{:S(2)}, u32[]{:S(2)}) collective-permute-start(bf16[1,32,2,1024]{3,2,1,0:T(2,128)(2,1)S(1)} %collective-permute-done.5), channel_id=1, source_target_pairs={{0,240},{16,0},{32,16},{48,32},{64,48},{80,64},{96,80},{112,96},{1... | collective-permute-start | bytes 393224 | tf_op jit(solution)/shard_map/ppermute | solution.py:21
  41.4 7.1 %collective-permute-start.6 = (bf16[1,32,2,1024]{3,2,1,0:T(2,128)(2,1)S(1)}, bf16[1,32,2,1024]{3,2,1,0:T(2,128)(2,1)S(1)}, u32[]{:S(2)}, u32[]{:S(2)}) collective-permute-start(bf16[1,32,2,1024]{3,2,1,0:T(2,128)(2,1)S(1)} %collective-permute-done.4), channel_id=1, source_target_pairs={{0,16},{16,32},{32,48},{48,64},{64,80},{80,96},{96,112},{112,128},... | collective-permute-start | bytes 393224 | tf_op jit(solution)/shard_map/ppermute | solution.py:18
  42.9 7.2 %collective-permute-start.9 = (bf16[1,32,2,1024]{3,2,1,0:T(2,128)(2,1)S(1)}, bf16[1,32,2,1024]{3,2,1,0:T(2,128)(2,1)S(1)}, u32[]{:S(2)}, u32[]{:S(2)}) collective-permute-start(bf16[1,32,2,1024]{3,2,1,0:T(2,128)(2,1)S(1)} %collective-permute-done.7), channel_id=1, source_target_pairs={{0,240},{16,0},{32,16},{48,32},{64,48},{80,64},{96,80},{112,96},{1... | collective-permute-start | bytes 393224 | tf_op jit(solution)/shard_map/ppermute | solution.py:21
  48.6 7.3 %collective-permute-start.8 = (bf16[1,32,2,1024]{3,2,1,0:T(2,128)(2,1)S(1)}, bf16[1,32,2,1024]{3,2,1,0:T(2,128)(2,1)S(1)}, u32[]{:S(2)}, u32[]{:S(2)}) collective-permute-start(bf16[1,32,2,1024]{3,2,1,0:T(2,128)(2,1)S(1)} %collective-permute-done.6), channel_id=1, source_target_pairs={{0,16},{16,32},{32,48},{48,64},{64,80},{80,96},{96,112},{112,128},... | collective-permute-start | bytes 393224 | tf_op jit(solution)/shard_map/ppermute | solution.py:18
  50.1 10.4 %collective-permute-start.11 = (bf16[1,32,2,1024]{3,2,1,0:T(2,128)(2,1)S(1)}, bf16[1,32,2,1024]{3,2,1,0:T(2,128)(2,1)S(1)}, u32[]{:S(2)}, u32[]{:S(2)}) collective-permute-start(bf16[1,32,2,1024]{3,2,1,0:T(2,128)(2,1)S(1)} %collective-permute-done.9), channel_id=1, source_target_pairs={{0,240},{16,0},{32,16},{48,32},{64,48},{80,64},{96,80},{112,96},{1... | collective-permute-start | bytes 393224 | tf_op jit(solution)/shard_map/ppermute | solution.py:21
  55.9 10.6 %collective-permute-start.10 = (bf16[1,32,2,1024]{3,2,1,0:T(2,128)(2,1)S(1)}, bf16[1,32,2,1024]{3,2,1,0:T(2,128)(2,1)S(1)}, u32[]{:S(2)}, u32[]{:S(2)}) collective-permute-start(bf16[1,32,2,1024]{3,2,1,0:T(2,128)(2,1)S(1)} %collective-permute-done.8), channel_id=1, source_target_pairs={{0,16},{16,32},{32,48},{48,64},{64,80},{80,96},{96,112},{112,128},... | collective-permute-start | bytes 393224 | tf_op jit(solution)/shard_map/ppermute | solution.py:18
  60.5 14.0 %collective-permute-start.13 = (bf16[1,32,2,1024]{3,2,1,0:T(2,128)(2,1)S(1)}, bf16[1,32,2,1024]{3,2,1,0:T(2,128)(2,1)S(1)}, u32[]{:S(2)}, u32[]{:S(2)}) collective-permute-start(bf16[1,32,2,1024]{3,2,1,0:T(2,128)(2,1)S(1)} %collective-permute-done.11), channel_id=1, source_target_pairs={{0,240},{16,0},{32,16},{48,32},{64,48},{80,64},{96,80},{112,96},{1... | collective-permute-start | bytes 393224 | tf_op jit(solution)/shard_map/ppermute | solution.py:21
  66.5 7.8 %collective-permute-start.12 = (bf16[1,32,2,1024]{3,2,1,0:T(2,128)(2,1)S(1)}, bf16[1,32,2,1024]{3,2,1,0:T(2,128)(2,1)S(1)}, u32[]{:S(2)}, u32[]{:S(2)}) collective-permute-start(bf16[1,32,2,1024]{3,2,1,0:T(2,128)(2,1)S(1)} %collective-permute-done.10), channel_id=1, source_target_pairs={{0,16},{16,32},{32,48},{48,64},{64,80},{80,96},{96,112},{112,128},... | collective-permute-start | bytes 393224 | tf_op jit(solution)/shard_map/ppermute | solution.py:18
  74.4 7.1 %collective-permute-start.14 = (bf16[1,32,2,1024]{3,2,1,0:T(2,128)(2,1)S(1)}, bf16[1,32,2,1024]{3,2,1,0:T(2,128)(2,1)S(1)}, u32[]{:S(2)}, u32[]{:S(2)}) collective-permute-start(bf16[1,32,2,1024]{3,2,1,0:T(2,128)(2,1)S(1)} %collective-permute-done.12), channel_id=1, source_target_pairs={{0,16},{16,32},{32,48},{48,64},{64,80},{80,96},{96,112},{112,128},... | collective-permute-start | bytes 393224 | tf_op jit(solution)/shard_map/ppermute | solution.py:18
  176.2 113.0 %all-to-all-start = ((bf16[16,4,2,128,128]{4,3,2,1,0:T(8,128)(2,1)}), bf16[16,4,2,128,128]{4,3,2,1,0:T(8,128)(2,1)}, u32[]{:S(2)}, u32[]{:S(2)}) async-start(bf16[16,4,2,128,128]{4,3,2,1,0:T(8,128)(2,1)} %get-tuple-element.28), calls=%async_computation | async-start | bytes 8388608 | tf_op jit(solution)/shard_map/all_to_all | solution.py:147
  305.5 54.5 %all-to-all-start.1 = ((f32[2,512,512]{2,0,1:T(2,128)}), f32[2,512,512]{2,0,1:T(2,128)S(1)}, u32[]{:S(2)}, u32[]{:S(2)}) async-start(f32[2,512,512]{2,0,1:T(2,128)} %reshape.352), calls=%async_computation.1 | async-start | bytes 4194304 | tf_op jit(solution)/shard_map/all_to_all | solution.py:166
  364.1 1.2 copy-start
Sparse Core Ops, SparseCore 0:
  15.4 55.3 all-gather.1
